TPU v7x, 32 devices: a whole 2x2x4 slice. The times are simulated.
32 devices in a mesh: parts: 2 (over y), blk: 4 (over z), grp: 4 (over x, core).
Axes of the slice: x: 2, y: 2, z: 4, core: 2. Of those that a mesh axis runs over, the one named last changes fastest.
Arguments:
- factors: float32 [64, 4096], P(None, ('parts', 'blk', 'grp')), parts along dimension 1, may hold values from -1 to 1
- tangent: float32 [64, 4096], P(None, ('parts', 'blk', 'grp')), parts along dimension 1, may hold values from -15 to 15
- counts: int32 [4096, 2048], P(('parts', 'blk', 'grp')), parts along dimension 0, may hold values from 0 to 4, as said below
Outputs:
- hess_vec: float32 [64, 4096], P(None, ('parts', 'blk', 'grp')), parts along dimension 1
- residual: float32 [64, 4096], P(None, ('parts', 'blk', 'grp')), parts along dimension 1
- inner: float32 [4], P('parts'), parts along dimension 0
There are 2 independent parts, one for each index of `parts`. A program takes and returns all parts, laid end to end along the dimension named above; each array names one. Nothing has to cross between parts.
Inputs may be any that keep to these rules, and one draw needn't show every extreme that they name: counts is symmetric.
All inputs are finite; a program needn't handle non-finite values.
Results may differ from a plain program's by a relative error of at most 0.0003.
Values sent between devices are 32-bit elements; how exact they have to be, the bound alone decides.
A program may use at most 128 MiB of HBM per device.

v0:
```python
import jax
import jax.numpy as jnp
from jax import lax
from jax.sharding import PartitionSpec as P


def local(factors, tangent, counts):
    rows = counts.shape[0]
    nodes = counts.shape[1]
    scale = 1.0 / jnp.sqrt(jnp.float32(nodes))
    highest = lax.Precision.HIGHEST
    contract = (((0,), (0,)), ((), ()))
    right = (((1,), (1,)), ((), ()))
    row_start = (lax.axis_index("blk") * lax.axis_size("grp") + lax.axis_index("grp")) * rows
    row_ids = row_start + jnp.arange(rows, dtype=jnp.int32)[:, None]
    group_u, group_v = (
        lax.all_gather(factors, "grp", axis=1, tiled=True),
        lax.all_gather(tangent, "grp", axis=1, tiled=True),
    )
    piece_u = lax.all_gather(group_u, "blk", axis=1, tiled=True)
    piece_v = lax.all_gather(group_v, "blk", axis=1, tiled=True)
    width = piece_u.shape[1]
    eta = lax.dot_general(factors, piece_u, contract, precision=highest)
    deta = lax.dot_general(factors, piece_v, contract, precision=highest) + lax.dot_general(
        tangent, piece_u, contract, precision=highest
    )
    col_ids = jnp.arange(width, dtype=jnp.int32)[None, :]
    keep = row_ids != col_ids
    rate = jnp.where(keep, jnp.exp(eta), jnp.float32(0.0))
    weight = rate * deta
    tile_counts = counts.astype(jnp.float32)
    slack = jnp.where(keep, tile_counts - rate, jnp.float32(0.0))
    hess_acc = lax.dot_general(piece_u, weight, right, precision=highest)
    resid_acc = lax.dot_general(piece_u, slack - weight, right, precision=highest)
    hess_acc, resid_acc = (hess_acc, resid_acc)
    hess_vec = hess_acc * scale
    residual = resid_acc * scale
    sum_sq, sum_curv = lax.psum(
        (jnp.sum(residual * residual), jnp.sum(tangent * hess_vec)), ("blk", "grp")
    )
    inner = jnp.stack([sum_sq, sum_curv])
    return (hess_vec, residual, inner)


def solution(mesh):
    return jax.shard_map(
        local,
        mesh=mesh,
        in_specs=(
            P(None, ("parts", "blk", "grp")),
            P(None, ("parts", "blk", "grp")),
            P(("parts", "blk", "grp"), None),
        ),
        out_specs=(P(None, ("parts", "blk", "grp")), P(None, ("parts", "blk", "grp")), P("parts")),
        check_vma=False,
    )
```

profile of v0, /device:TPU:0, one launch (start us, length us, event | category | flops | bytes accessed | tf_op | source)
XLA Modules:
  0.0 85.9 jit_solution(17943244656120877728)
XLA Ops:
  0.6 0.0 copy-start.1
  0.7 6.7 %all_gather.12 = f32[64,512]{1,0:T(8,128)S(1)} all-gather(f32[64,128]{1,0:T(8,128)} %param.3), channel_id=1, replica_groups=mesh['parts'=2,'blk'=4,'grp'=4] {'grp'}, dimensions={1}, use_global_device_ids=true | all-gather | bytes 163840 | tf_op jit(solution)/shard_map/all_gather | solution.py:17
  7.4 0.0 copy-done.1
  7.4 5.6 %all_gather.14 = f32[64,512]{1,0:T(8,128)S(1)} all-gather(f32[64,128]{1,0:T(8,128)S(1)} %copy-done.1), channel_id=1, replica_groups=mesh['parts'=2,'blk'=4,'grp'=4] {'grp'}, dimensions={1}, use_global_device_ids=true | all-gather | bytes 163840 | tf_op jit(solution)/shard_map/all_gather | solution.py:18
  12.9 16.6 %all_gather.13 = f32[64,2048]{1,0:T(8,128)S(1)} all-gather(f32[64,512]{1,0:T(8,128)S(1)} %all_gather.12), channel_id=1, replica_groups=mesh['parts'=2,'blk'=4,'grp'=4] {'blk'}, dimensions={1}, use_global_device_ids=true | all-gather | bytes 655360 | tf_op jit(solution)/shard_map/all_gather | solution.py:20
  29.5 0.0 copy-start.2
  29.5 16.0 %all_gather.15 = f32[64,2048]{1,0:T(8,128)S(1)} all-gather(f32[64,512]{1,0:T(8,128)S(1)} %all_gather.14), channel_id=1, replica_groups=mesh['parts'=2,'blk'=4,'grp'=4] {'blk'}, dimensions={1}, use_global_device_ids=true | all-gather | bytes 655360 | tf_op jit(solution)/shard_map/all_gather | solution.py:21
  45.5 0.0 copy-done.2
  45.5 1.0 %fusion.11 = f32[128,2048]{1,0:T(8,128)S(1)} fusion(f32[64,128]{1,0:T(8,128)S(1)} %copy-done.2, f32[64,2048]{1,0:T(8,128)S(1)} %all_gather.15), kind=kOutput, calls=%fused_computation.20 | convolution fusion | flops 201326592 | bytes 1605632 | tf_op jit(solution)/shard_map/dot_general | solution.py:24
  46.6 1.1 %fusion.1 = f32[128,2048]{1,0:T(8,128)S(1)} fusion(f32[64,128]{1,0:T(8,128)S(1)} %copy-done.2, f32[64,2048]{1,0:T(8,128)S(1)} %all_gather.13, s32[128]{0:T(128)S(1)} %iota_add_fusion), kind=kOutput, calls=%fused_computation.3 | convolution fusion | flops 201850880 | bytes 1606144 | tf_op jit(solution)/shard_map/dot_general | solution.py:23
  47.7 0.0 copy-start
  47.7 1.1 %fusion = f32[128,2048]{1,0:T(8,128)S(1)} fusion(f32[128,2048]{1,0:T(8,128)S(1)} %fusion.1, f32[128,2048]{1,0:T(8,128)S(1)} %fusion.11, f32[64,128]{1,0:T(8,128)S(1)} %copy-done.1, f32[64,2048]{1,0:T(8,128)S(1)} %all_gather.13), kind=kOutput, calls=%fused_computation.1 | convolution fusion | flops 201850880 | bytes 3702784 | tf_op jit(solution)/shard_map/dot_general | solution.py:24
  48.8 0.2 copy-done
  48.9 2.7 %multiply_reduce_fusion.1 = (f32[]{:T(128)}, f32[64,128]{1,0:T(8,128)}) fusion(f32[64,2048]{1,0:T(8,128)S(1)} %all_gather.13, f32[128,2048]{1,0:T(8,128)S(1)} %fusion, f32[128,2048]{1,0:T(8,128)S(1)} %fusion.1, s32[128,2048]{1,0:T(8,128)S(1)} %copy-done, s32[128]{0:T(128)S(1)} %iota_add_fusion), kind=kOutput, calls=%fused_computation.16 | convolution fusion | flops 202661888 | bytes 3703300 | tf_op jit(solution)/shard_map/dot_general | solution.py:34
  51.6 2.4 %multiply_reduce_fusion = (f32[]{:T(128)}, f32[64,128]{1,0:T(8,128)}) fusion(f32[64,128]{1,0:T(8,128)S(1)} %copy-done.1, f32[128,2048]{1,0:T(8,128)S(1)} %fusion, f32[64,2048]{1,0:T(8,128)S(1)} %all_gather.13), kind=kOutput, calls=%fused_computation.15 | convolution fusion | flops 201351168 | bytes 1638404 | tf_op jit(solution)/shard_map/dot_general | solution.py:33
  54.0 30.1 %all-reduce = (f32[1]{0:T(128)}, f32[1]{0:T(128)}) all-reduce(f32[1]{0:T(128)} %bitcast.3, f32[1]{0:T(128)} %bitcast.2), channel_id=1, replica_groups=mesh['parts'=2,'blk'=4,'grp'=4] {'blk','grp'}, use_global_device_ids=true, to_apply=%region_3.4 | all-reduce | flops 2 | bytes 16 | tf_op jit(solution)/shard_map/psum | solution.py:38
  84.2 1.8 %pad_maximum_fusion = f32[2]{0:T(128)} fusion(f32[1]{0:T(128)} %get-tuple-element.3, f32[1]{0:T(128)} %get-tuple-element.4), kind=kLoop, calls=%fused_computation.17 | loop fusion | flops 2 | bytes 16 | tf_op jit(solution)/shard_map/stack | solution.py:41
  (1 shorter events, 0.0 us)
Async XLA Ops:
  0.6 6.7 %copy-start.1 = (f32[64,128]{1,0:T(8,128)S(1)}, f32[64,128]{1,0:T(8,128)}, u32[]{:S(2)}) copy-start(f32[64,128]{1,0:T(8,128)} %param.4) | copy-start | bytes 98308
  29.5 16.0 %copy-start.2 = (f32[64,128]{1,0:T(8,128)S(1)}, f32[64,128]{1,0:T(8,128)}, u32[]{:S(2)}) copy-start(f32[64,128]{1,0:T(8,128)} %param.3) | copy-start | bytes 98308
  47.7 1.2 %copy-start = (s32[128,2048]{1,0:T(8,128)S(1)}, s32[128,2048]{1,0:T(8,128)}, u32[]{:S(2)}) copy-start(s32[128,2048]{1,0:T(8,128)} %param.5) | copy-start | bytes 3145732
where the time goes:
time: 86.3 us; the launch traced here: 85.9 us
  blocking collectives  75 us (87%)
  matrix products  8.3 us (10%)
  other arithmetic  1.78 us (2%)
    psum x1, blocking collectives, local(): lax.psum((jnp.sum(residual * residual), jnp.sum(tangent * hess_vec)), ('b...  30.1 us
    all_gather x1, blocking collectives, local(): piece_u = lax.all_gather(group_u, 'blk', axis=1, tiled=True)  16.6 us
    all_gather x1, blocking collectives, local(): piece_v = lax.all_gather(group_v, 'blk', axis=1, tiled=True)  16 us
    all_gather x1, blocking collectives, local(): lax.all_gather(factors, 'grp', axis=1, tiled=True)  6.69 us
    all_gather x1, blocking collectives, local(): lax.all_gather(tangent, 'grp', axis=1, tiled=True)  5.58 us
    dot_general x1, matrix products, local(): lax.dot_general(piece_u, slack - weight, right, precision=highest)  2.69 us
    dot_general x1, matrix products, local(): hess_acc = lax.dot_general(piece_u, weight, right, precision=highest)  2.41 us
    another operation x1, other arithmetic, local(): inner = jnp.stack([sum_sq, sum_curv])  1.78 us

commit v1 on v0

--- a/solution.py
+++ b/solution.py
@@ -1,7 +1,17 @@
+import functools
 import jax
 import jax.numpy as jnp
 from jax import lax
 from jax.sharding import PartitionSpec as P
+
+
+def _produce_limits(x_local, axis_key, mesh_ax):
+    w2 = jax.lax.psum(x_local, axis_name=axis_key)
+    base_arr = jax.lax.psum(w2, axis_name=mesh_ax)
+    return base_arr
+
+
+shape_slot_on_mesh = functools.partial(_produce_limits, axis_key="grp", mesh_ax="blk")
 
 
 def local(factors, tangent, counts):
@@ -35,8 +45,8 @@
     hess_acc, resid_acc = (hess_acc, resid_acc)
     hess_vec = hess_acc * scale
     residual = resid_acc * scale
-    sum_sq, sum_curv = lax.psum(
-        (jnp.sum(residual * residual), jnp.sum(tangent * hess_vec)), ("blk", "grp")
+    sum_sq, sum_curv = shape_slot_on_mesh(
+        (jnp.sum(residual * residual), jnp.sum(tangent * hess_vec))
     )
     inner = jnp.stack([sum_sq, sum_curv])
     return (hess_vec, residual, inner)

time: 86.3 us -> 74.4 us (0.86)
  blocking collectives: 75 us -> 63.2 us
    psum x1 -> x2, blocking collectives: 30.1 us -> 18.3 us  [the longest x1 12 us: _produce_limits(): base_arr = jax.lax.psum(w2, axis_name=mesh_ax)]
where the time goes in v1:
time: 74.4 us; the launch traced here: 74 us
  blocking collectives  63.2 us (85%)
  matrix products  8.22 us (11%)
  other arithmetic  1.78 us (2%)
    all_gather x1, blocking collectives, local(): piece_u = lax.all_gather(group_u, 'blk', axis=1, tiled=True)  16.6 us
    all_gather x1, blocking collectives, local(): piece_v = lax.all_gather(group_v, 'blk', axis=1, tiled=True)  16 us
    psum x1, blocking collectives, _produce_limits(): base_arr = jax.lax.psum(w2, axis_name=mesh_ax)  12 us
    all_gather x1, blocking collectives, local(): lax.all_gather(factors, 'grp', axis=1, tiled=True)  6.69 us
    psum x1, blocking collectives, _produce_limits(): w2 = jax.lax.psum(x_local, axis_name=axis_key)  6.35 us
    all_gather x1, blocking collectives, local(): lax.all_gather(tangent, 'grp', axis=1, tiled=True)  5.58 us
    dot_general x1, matrix products, local(): lax.dot_general(piece_u, slack - weight, right, precision=highest)  2.6 us
    dot_general x1, matrix products, local(): hess_acc = lax.dot_general(piece_u, weight, right, precision=highest)  2.41 us

profile of v1, /device:TPU:0, one launch (start us, length us, event | category | flops | bytes accessed | tf_op | source)
XLA Modules:
  0.0 74.0 jit_solution(2162573603261192260)
XLA Ops:
  0.6 0.0 copy-start.1
  0.7 6.7 %all_gather.12 = f32[64,512]{1,0:T(8,128)S(1)} all-gather(f32[64,128]{1,0:T(8,128)} %param.3), channel_id=1, replica_groups=mesh['parts'=2,'blk'=4,'grp'=4] {'grp'}, dimensions={1}, use_global_device_ids=true | all-gather | bytes 163840 | tf_op jit(solution)/shard_map/all_gather | solution.py:27
  7.4 0.0 copy-done.1
  7.4 5.6 %all_gather.14 = f32[64,512]{1,0:T(8,128)S(1)} all-gather(f32[64,128]{1,0:T(8,128)S(1)} %copy-done.1), channel_id=1, replica_groups=mesh['parts'=2,'blk'=4,'grp'=4] {'grp'}, dimensions={1}, use_global_device_ids=true | all-gather | bytes 163840 | tf_op jit(solution)/shard_map/all_gather | solution.py:28
  12.9 16.6 %all_gather.13 = f32[64,2048]{1,0:T(8,128)S(1)} all-gather(f32[64,512]{1,0:T(8,128)S(1)} %all_gather.12), channel_id=1, replica_groups=mesh['parts'=2,'blk'=4,'grp'=4] {'blk'}, dimensions={1}, use_global_device_ids=true | all-gather | bytes 655360 | tf_op jit(solution)/shard_map/all_gather | solution.py:30
  29.5 0.0 copy-start.2
  29.5 16.0 %all_gather.15 = f32[64,2048]{1,0:T(8,128)S(1)} all-gather(f32[64,512]{1,0:T(8,128)S(1)} %all_gather.14), channel_id=1, replica_groups=mesh['parts'=2,'blk'=4,'grp'=4] {'blk'}, dimensions={1}, use_global_device_ids=true | all-gather | bytes 655360 | tf_op jit(solution)/shard_map/all_gather | solution.py:31
  45.5 0.0 copy-done.2
  45.5 1.0 %fusion.11 = f32[128,2048]{1,0:T(8,128)S(1)} fusion(f32[64,128]{1,0:T(8,128)S(1)} %copy-done.2, f32[64,2048]{1,0:T(8,128)S(1)} %all_gather.15), kind=kOutput, calls=%fused_computation.20 | convolution fusion | flops 201326592 | bytes 1605632 | tf_op jit(solution)/shard_map/dot_general | solution.py:34
  46.6 1.1 %fusion.1 = f32[128,2048]{1,0:T(8,128)S(1)} fusion(f32[64,128]{1,0:T(8,128)S(1)} %copy-done.2, f32[64,2048]{1,0:T(8,128)S(1)} %all_gather.13, s32[128]{0:T(128)S(1)} %iota_add_fusion), kind=kOutput, calls=%fused_computation.3 | convolution fusion | flops 201850880 | bytes 1606144 | tf_op jit(solution)/shard_map/dot_general | solution.py:33
  47.7 0.0 copy-start
  47.7 1.1 %fusion = f32[128,2048]{1,0:T(8,128)S(1)} fusion(f32[128,2048]{1,0:T(8,128)S(1)} %fusion.1, f32[128,2048]{1,0:T(8,128)S(1)} %fusion.11, f32[64,128]{1,0:T(8,128)S(1)} %copy-done.1, f32[64,2048]{1,0:T(8,128)S(1)} %all_gather.13), kind=kOutput, calls=%fused_computation.1 | convolution fusion | flops 201850880 | bytes 3702784 | tf_op jit(solution)/shard_map/dot_general | solution.py:34
  48.8 0.2 copy-done
  48.9 2.6 %multiply_reduce_fusion.1 = (f32[]{:T(128)}, f32[64,128]{1,0:T(8,128)}) fusion(f32[64,2048]{1,0:T(8,128)S(1)} %all_gather.13, f32[128,2048]{1,0:T(8,128)S(1)} %fusion, f32[128,2048]{1,0:T(8,128)S(1)} %fusion.1, s32[128,2048]{1,0:T(8,128)S(1)} %copy-done, s32[128]{0:T(128)S(1)} %iota_add_fusion), kind=kOutput, calls=%fused_computation.16 | convolution fusion | flops 202661888 | bytes 3703300 | tf_op jit(solution)/shard_map/dot_general | solution.py:44
  51.5 2.4 %multiply_reduce_fusion = (f32[]{:T(128)}, f32[64,128]{1,0:T(8,128)}) fusion(f32[64,128]{1,0:T(8,128)S(1)} %copy-done.1, f32[128,2048]{1,0:T(8,128)S(1)} %fusion, f32[64,2048]{1,0:T(8,128)S(1)} %all_gather.13), kind=kOutput, calls=%fused_computation.15 | convolution fusion | flops 201351168 | bytes 1638404 | tf_op jit(solution)/shard_map/dot_general | solution.py:43
  53.9 6.3 %all-reduce = (f32[]{:T(128)}, f32[]{:T(128)}) all-reduce(f32[]{:T(128)} %get-tuple-element.7, f32[]{:T(128)} %get-tuple-element.9), channel_id=1, replica_groups=mesh['parts'=2,'blk'=4,'grp'=4] {'grp'}, use_global_device_ids=true, to_apply=%region_4.5 | all-reduce | flops 2 | bytes 16 | tf_op jit(solution)/shard_map/psum | solution.py:9
  60.3 12.0 %all-reduce.1 = (f32[1]{0:T(128)}, f32[1]{0:T(128)}) all-reduce(f32[1]{0:T(128)} %bitcast.3, f32[1]{0:T(128)} %bitcast.2), channel_id=1, replica_groups=mesh['parts'=2,'blk'=4,'grp'=4] {'blk'}, use_global_device_ids=true, to_apply=%region_5.6 | all-reduce | flops 2 | bytes 16 | tf_op jit(solution)/shard_map/psum | solution.py:10
  72.3 1.8 %pad_maximum_fusion = f32[2]{0:T(128)} fusion(f32[1]{0:T(128)} %get-tuple-element.5, f32[1]{0:T(128)} %get-tuple-element.6), kind=kLoop, calls=%fused_computation.17 | loop fusion | flops 2 | bytes 16 | tf_op jit(solution)/shard_map/stack | solution.py:51
  (1 shorter events, 0.0 us)
Async XLA Ops:
  0.6 6.7 %copy-start.1 = (f32[64,128]{1,0:T(8,128)S(1)}, f32[64,128]{1,0:T(8,128)}, u32[]{:S(2)}) copy-start(f32[64,128]{1,0:T(8,128)} %param.4) | copy-start | bytes 98308
  29.5 16.0 %copy-start.2 = (f32[64,128]{1,0:T(8,128)S(1)}, f32[64,128]{1,0:T(8,128)}, u32[]{:S(2)}) copy-start(f32[64,128]{1,0:T(8,128)} %param.3) | copy-start | bytes 98308
  47.7 1.2 %copy-start = (s32[128,2048]{1,0:T(8,128)S(1)}, s32[128,2048]{1,0:T(8,128)}, u32[]{:S(2)}) copy-start(s32[128,2048]{1,0:T(8,128)} %param.5) | copy-start | bytes 3145732
